TPU v7x, 512 devices: a whole 4x8x8 slice. The times are simulated.
512 devices in a mesh: ep: 128 (over y, z, core), dp: 4 (over x).
Axes of the slice: x: 4, y: 8, z: 8, core: 2. Of those that a mesh axis runs over, the one named last changes fastest.
Arguments:
- activations: float32 [256, 256, 768], P('ep', 'dp'), may hold values from -6 to 6
- out_grads: float32 [256, 256, 512], P('ep', 'dp'), may hold values from -6 to 6
- counts: int32 [256, 4], P('ep', 'dp'), may hold values from 1 to 64
- slot_weights: float32 [256, 768, 512], P('ep', None, 'dp'), may hold values from -0.21875 to 0.21875
- master: float32 [128, 768, 512], P(None, 'ep', 'dp'), may hold values from -0.21875 to 0.21875
- moment_one: float32 [128, 768, 512], P(None, 'ep', 'dp'), may hold values from -6 to 6
- moment_two: float32 [128, 768, 512], P(None, 'ep', 'dp'), may hold values from 1 to 100
- old_table: int32 [256, 1], replicated, may hold values from 0 to 127
- new_table: int32 [256, 1], replicated, may hold values from 0 to 127
Outputs:
- outputs: float32 [256, 256, 512], P('ep', 'dp')
- input_grads: float32 [256, 256, 768], P('ep', 'dp')
- new_master: float32 [128, 768, 512], P(None, 'ep', 'dp')
- new_moment_one: float32 [128, 768, 512], P(None, 'ep', 'dp')
- new_moment_two: float32 [128, 768, 512], P(None, 'ep', 'dp')
- new_slots: float32 [256, 768, 512], P('ep', None, 'dp')
Inputs may be any that keep to these rules, and one draw needn't show every extreme that they name: `old_table`: every expert is named by at least one old slot. `new_table`: every expert is named by at least one new slot.
All inputs are finite; a program needn't handle non-finite values.
Results may differ from a plain program's by a relative error of at most 0.00007.
Values sent between devices are 32-bit elements; how exact they have to be, the bound alone decides.
No kernel may reach another device: no remote copies, remote signals or barrier semaphores. Data moves between devices by JAX's collectives and lax.ppermute only.
A program may use at most 64 MiB of HBM per device.

v0:
```python
import jax
import jax.numpy as jnp
from jax import lax
from jax.sharding import PartitionSpec as P

STEP = 100
beta_one = 0.9
beta_two = 0.999
learn_rate = 0.02
epsilon = 1e-08
decay_rate = 0.1


def adamw(master, moment_one, moment_two, expert_grad):
    first_new = beta_one * moment_one + (1.0 - beta_one) * expert_grad
    second_new = beta_two * moment_two + (1.0 - beta_two) * expert_grad * expert_grad
    first_hat = first_new / (1.0 - beta_one**STEP)
    second_hat = second_new / (1.0 - beta_two**STEP)
    updated = master - learn_rate * (
        first_hat / (jnp.sqrt(second_hat) + epsilon) + decay_rate * master
    )
    return (updated, first_new, second_new)


def local(
    activations,
    out_grads,
    counts,
    slot_weights,
    master,
    moment_one,
    moment_two,
    old_table,
    new_table,
):
    precise = lax.Precision.HIGHEST
    experts_ids = jnp.arange(master.shape[0], dtype=jnp.int32)
    old_onehot = (old_table[:, 0][None, :] == experts_ids[:, None]).astype(jnp.float32)
    positions = jnp.arange(activations.shape[1], dtype=jnp.int32)
    live_rows = (positions[None, :] < counts).astype(jnp.float32)
    masked_acts = activations * live_rows[:, :, None]
    masked_grads = out_grads * live_rows[:, :, None]
    whole_weights = lax.all_gather(slot_weights, "dp", axis=2, tiled=True)
    outputs = jnp.einsum("srf,sfd->srd", masked_acts, whole_weights, precision=precise)
    input_grads = jnp.einsum("srd,sfd->srf", masked_grads, whole_weights, precision=precise)
    every_act = lax.all_gather(masked_acts, "dp", axis=1, tiled=True)
    own_columns = lax.all_to_all(masked_grads, "dp", split_axis=2, concat_axis=1, tiled=True)
    column_grad = jnp.einsum("srf,srd->sfd", every_act, own_columns, precision=precise)
    arrived = lax.all_to_all(column_grad, "ep", split_axis=1, concat_axis=0, tiled=True)
    expert_grad = jnp.einsum("es,sfd->efd", old_onehot, arrived, precision=precise)
    new_master, new_moment_one, new_moment_two = adamw(master, moment_one, moment_two, expert_grad)
    new_onehot = (new_table[:, 0][:, None] == experts_ids[None, :]).astype(jnp.float32)
    picked = jnp.einsum("se,efd->sfd", new_onehot, new_master, precision=precise)
    new_slots = lax.all_to_all(picked, "ep", split_axis=0, concat_axis=1, tiled=True)
    return (outputs, input_grads, new_master, new_moment_one, new_moment_two, new_slots)


def solution(mesh):
    in_specs = (
        P("ep", "dp", None),
        P("ep", "dp", None),
        P("ep", "dp"),
        P("ep", None, "dp"),
        P(None, "ep", "dp"),
        P(None, "ep", "dp"),
        P(None, "ep", "dp"),
        P(),
        P(),
    )
    out_specs = (
        P("ep", "dp", None),
        P("ep", "dp", None),
        P(None, "ep", "dp"),
        P(None, "ep", "dp"),
        P(None, "ep", "dp"),
        P("ep", None, "dp"),
    )
    return jax.shard_map(local, mesh=mesh, in_specs=in_specs, out_specs=out_specs, check_vma=False)
```

profile of v0, /device:TPU:8, one launch (start us, length us, event | category | flops | bytes accessed | tf_op | source)
XLA Modules:
  0.0 141.4 jit_solution(7682760392878343886)
XLA Ops:
  7.2 0.7 compare_convert_fusion
  7.9 1.8 %broadcast_multiply_fusion = f32[2,64,768]{2,1,0:T(8,128)} fusion(f32[2,64,768]{2,1,0:T(8,128)} %param.9, f32[2,64]{1,0:T(2,128)S(1)} %compare_convert_fusion), kind=kLoop, calls=%fused_computation.4 | loop fusion | flops 98304 | bytes 786944 | tf_op jit(solution)/shard_map/mul | solution.py:41
  9.8 0.7 all-gather.3.cloned.1.call-update
  10.5 1.0 broadcast_multiply_fusion.1
  11.6 0.2 copy.31
  11.8 0.6 reshape.38
  12.4 10.8 %all_to_all.54 = f32[4,1,16384]{2,1,0:T(1,128)S(1)} all-to-all(f32[4,1,16384]{2,1,0:T(1,128)S(1)} %reshape.38), channel_id=1, replica_groups=mesh['ep'=128,'dp'=4] {'dp'}, dimensions={0} | all-to-all | bytes 524288 | tf_op jit(solution)/shard_map/all_to_all | solution.py:47
  23.2 0.5 broadcast.23
  23.7 1.4 reduce
  25.1 0.4 reshape.39
  25.7 21.4 %all-gather.5.cloned.1.call-done = f32[2,256,768]{2,1,0:T(8,128)} async-done(((f32[2,64,768]{2,1,0:T(8,128)}), f32[2,256,768]{2,1,0:T(8,128)}) %all-gather.5.cloned.1.call-update) | async-done | bytes 1572880 | tf_op jit(solution)/shard_map/all_gather | solution.py:46
  47.1 4.1 %fusion.12 = f32[2,768,128]{2,1,0:T(8,128)S(1)} fusion(f32[2,256,768]{2,1,0:T(8,128)} %all-gather.5.cloned.1.call-done, f32[2,256,128]{2,1,0:T(8,128)S(1)} %bitcast.39), kind=kOutput, calls=%fused_computation.17 | convolution fusion | flops 603979776 | bytes 2621440 | tf_op jit(solution)/shard_map/srf,srd->sfd/dot_general | solution.py:48
  51.3 0.6 copy.33
  51.9 39.8 %all_to_all.55 = f32[2,768,128]{2,0,1:T(2,128)S(1)} all-to-all(f32[2,768,128]{2,0,1:T(2,128)S(1)} %copy.33), channel_id=1, replica_groups=mesh['ep'=128,'dp'=4] {'ep'}, dimensions={1} | all-to-all | bytes 1572864 | tf_op jit(solution)/shard_map/all_to_all | solution.py:49
  91.7 0.3 copy.34
  92.0 1.5 %multiply_subtract_fusion = (f32[128,6,128]{2,0,1:T(8,128)S(1)}, f32[128,6,128]{2,0,1:T(8,128)}, f32[128,6,128]{2,0,1:T(8,128)}) fusion(f32[128,6,128]{2,0,1:T(8,128)S(1)} %copy-done.3, f32[128,6,128]{2,0,1:T(8,128)S(1)} %copy-done.4, f32[128,6,128]{2,0,1:T(8,128)S(1)} %copy-done.5, f32[256,6,128]{2,0,1:T(8,128)S(1)} %bitcast.36, s32[256]{0:T(256)S(1)} %bitcast.40), kind=kOutput, calls=%fused_computation.2 | convolution fusion | flops 303497216 | bytes 3146752 | tf_op jit(solution)/shard_map/es,sfd->efd/dot_general | solution.py:50
  93.6 0.5 fusion.5
  94.1 1.5 %copy.35 = f32[256,6,128]{2,1,0:T(8,128)} copy(f32[256,6,128]{2,0,1:T(8,128)S(1)} %fusion.5) | data formatting | bytes 1572864 | tf_op jit(solution)/shard_map/se,efd->sfd/dot_general | solution.py:53
  95.6 6.2 %all-to-all-start.2 = ((f32[256,6,128]{2,1,0:T(8,128)}), f32[256,6,128]{2,1,0:T(8,128)S(1)}, u32[]{:S(2)}, u32[]{:S(2)}) async-start(f32[256,6,128]{2,1,0:T(8,128)} %copy.35), calls=%async_computation.2 | async-start | bytes 2097152 | tf_op jit(solution)/shard_map/all_to_all | solution.py:54
  101.8 4.8 %fusion.10 = f32[2,64,512]{2,1,0:T(8,128)} fusion(f32[2,64,768]{2,1,0:T(8,128)S(1)} %copy-done.1, f32[2,768,512]{2,1,0:T(8,128)} %all-gather.3.cloned.1.call-done), kind=kOutput, calls=%fused_computation.15 | convolution fusion | flops 603979776 | bytes 3801088 | tf_op jit(solution)/shard_map/srf,sfd->srd/dot_general | solution.py:44
  106.6 3.9 %fusion.11 = f32[2,64,768]{2,1,0:T(8,128)} fusion(f32[2,64,512]{2,1,0:T(8,128)S(1)} %broadcast_multiply_fusion.1, f32[2,768,512]{2,1,0:T(8,128)S(1)} %copy-done), kind=kOutput, calls=%fused_computation.16 | convolution fusion | flops 603979776 | bytes 3801088 | tf_op jit(solution)/shard_map/srd,sfd->srf/dot_general | solution.py:45
  110.5 22.7 %all-to-all-done.2 = f32[256,6,128]{2,1,0:T(8,128)S(1)} async-done(((f32[256,6,128]{2,1,0:T(8,128)}), f32[256,6,128]{2,1,0:T(8,128)S(1)}, u32[]{:S(2)}, u32[]{:S(2)}) %all-to-all-start.2) | async-done | bytes 786464 | tf_op jit(solution)/shard_map/all_to_all | solution.py:54
  133.2 0.4 copy.36
  133.6 0.9 copy.37
  (21 shorter events, 0.3 us)
Async XLA Ops:
  7.2 40.0 %all-gather.5.cloned.1.call-start = ((), (), s32[]{:S(2)}) async-start(), calls=%async_computation.4 | async-start | bytes 1966080 | tf_op jit(solution)/shard_map/all_gather | solution.py:46
  9.8 92.0 %all-gather.3.cloned.1.call-start = ((), (), s32[]{:S(2)}) async-start(), calls=%async_computation.3 | async-start | bytes 3932160 | tf_op jit(solution)/shard_map/all_gather | solution.py:43
  47.1 44.9 %copy-start.3 = (f32[128,6,128]{2,0,1:T(8,128)S(1)}, f32[128,6,128]{2,0,1:T(8,128)}, u32[]{:S(2)}) copy-start(f32[128,6,128]{2,0,1:T(8,128)} %param.13) | copy-start | bytes 1179652
  47.1 44.9 %copy-start.4 = (f32[128,6,128]{2,0,1:T(8,128)S(1)}, f32[128,6,128]{2,0,1:T(8,128)}, u32[]{:S(2)}) copy-start(f32[128,6,128]{2,0,1:T(8,128)} %param.14) | copy-start | bytes 1179652
  47.1 44.9 %copy-start.5 = (f32[128,6,128]{2,0,1:T(8,128)S(1)}, f32[128,6,128]{2,0,1:T(8,128)}, u32[]{:S(2)}) copy-start(f32[128,6,128]{2,0,1:T(8,128)} %param.15) | copy-start | bytes 1179652
  47.1 44.9 %copy-start.6 = (s32[256,1]{0,1:T(1,128)S(1)}, s32[256,1]{0,1:T(1,128)}, u32[]{:S(2)}) copy-start(s32[256,1]{0,1:T(1,128)} %param.16) | copy-start | bytes 3076
  51.9 41.7 %copy-start.7 = (s32[256,1]{0,1:T(1,128)S(1)}, s32[256,1]{0,1:T(1,128)}, u32[]{:S(2)}) copy-start(s32[256,1]{0,1:T(1,128)} %param.17) | copy-start | bytes 3076
  93.6 13.0 %copy-start.2 = (f32[128,6,128]{2,0,1:T(8,128)}, f32[128,6,128]{2,0,1:T(8,128)S(1)}, u32[]{:S(2)}) copy-start(f32[128,6,128]{2,0,1:T(8,128)S(1)} %get-tuple-element.24) | copy-start | bytes 1179652
  93.6 8.2 %copy-start.1 = (f32[2,64,768]{2,1,0:T(8,128)S(1)}, f32[2,64,768]{2,1,0:T(8,128)}, u32[]{:S(2)}) copy-start(f32[2,64,768]{2,1,0:T(8,128)} %broadcast_multiply_fusion) | copy-start | bytes 1179652
  95.6 37.6 %all-to-all-start.2 = ((f32[256,6,128]{2,1,0:T(8,128)}), f32[256,6,128]{2,1,0:T(8,128)S(1)}, u32[]{:S(2)}, u32[]{:S(2)}) async-start(f32[256,6,128]{2,1,0:T(8,128)} %copy.35), calls=%async_computation.2 | async-start | bytes 2097152 | tf_op jit(solution)/shard_map/all_to_all | solution.py:54
  101.8 4.8 %copy-start = (f32[2,768,512]{2,1,0:T(8,128)S(1)}, f32[2,768,512]{2,1,0:T(8,128)}, u32[]{:S(2)}) copy-start(f32[2,768,512]{2,1,0:T(8,128)} %all-gather.3.cloned.1.call-done) | copy-start | bytes 9437188
Sparse Core Ops, SparseCore 0:
  10.7 36.4 all-gather.4
  49.2 48.6 all-gather.2
where the time goes:
time: 142 us; the launch traced here: 141 us
  blocking collectives  50.6 us (36%)
  waiting for transfers between devices  44.9 us (32%)
  matrix products  14.8 us (10%)
  between operations  14.2 us (10%)
  starting transfers between devices  6.29 us (4%)
  local copies, waits for them, and re-layouts  5.63 us (4%)
  other arithmetic  4.96 us (3%)
    all_to_all x1, blocking collectives, local(): lax.all_to_all(column_grad, 'ep', split_axis=1, concat_axis=0, tiled=True)  39.8 us
    all_to_all x1, waiting for transfers between devices, local(): lax.all_to_all(picked, 'ep', split_axis=0, concat_axis=1, tiled=True)  22.7 us
    all_gather x1, waiting for transfers between devices, local(): every_act = lax.all_gather(masked_acts, 'dp', axis=1, tiled=True)  21.4 us
    all_to_all x1, blocking collectives, local(): lax.all_to_all(masked_grads, 'dp', split_axis=2, concat_axis=1, tiled=True)  10.8 us
    all_to_all x1, starting transfers between devices, local(): lax.all_to_all(picked, 'ep', split_axis=0, concat_axis=1, tiled=True)  6.21 us
    dot_general x1, matrix products, local(): jnp.einsum('srf,sfd->srd', masked_acts, whole_weights, precision=precise)  4.76 us
    dot_general x1, matrix products, local(): jnp.einsum('srf,srd->sfd', every_act, own_columns, precision=precise)  4.13 us
    dot_general x1, matrix products, local(): jnp.einsum('srd,sfd->srf', masked_grads, whole_weights, precision=precise)  3.89 us
  transfers between devices with their start and end apart: 3, of which 2 were waited for; matrix products, arithmetic and copies ran while one was open for 15% of the time, Pallas kernels for 0%

commit v1 on v0

--- a/solution.py
+++ b/solution.py
@@ -43,9 +43,39 @@
     whole_weights = lax.all_gather(slot_weights, "dp", axis=2, tiled=True)
     outputs = jnp.einsum("srf,sfd->srd", masked_acts, whole_weights, precision=precise)
     input_grads = jnp.einsum("srd,sfd->srf", masked_grads, whole_weights, precision=precise)
-    every_act = lax.all_gather(masked_acts, "dp", axis=1, tiled=True)
     own_columns = lax.all_to_all(masked_grads, "dp", split_axis=2, concat_axis=1, tiled=True)
-    column_grad = jnp.einsum("srf,srd->sfd", every_act, own_columns, precision=precise)
+    size, index, span = (lax.axis_size("dp"), lax.axis_index("dp"), masked_acts.shape[1])
+    ahead = [(i, (i + 1) % size) for i in range(size)]
+    downward = [(i, (i - 1) % size) for i in range(size)]
+    middle = size // 2
+    from_left = from_right = masked_acts
+    total = jnp.einsum(
+        "srf,srd->sfd",
+        masked_acts,
+        lax.dynamic_slice_in_dim(own_columns, index * span, masked_acts.shape[1], axis=1),
+        precision=precise,
+    )
+    for lap in range(1, middle + 1):
+        from_left = lax.ppermute(from_left, "dp", ahead)
+        if lap < size - middle:
+            from_right = lax.ppermute(from_right, "dp", downward)
+            total = total + jnp.einsum(
+                "srf,srd->sfd",
+                from_right,
+                lax.dynamic_slice_in_dim(
+                    own_columns, (index + lap) % size * span, from_right.shape[1], axis=1
+                ),
+                precision=precise,
+            )
+        total = total + jnp.einsum(
+            "srf,srd->sfd",
+            from_left,
+            lax.dynamic_slice_in_dim(
+                own_columns, (index - lap) % size * span, from_left.shape[1], axis=1
+            ),
+            precision=precise,
+        )
+    column_grad = total
     arrived = lax.all_to_all(column_grad, "ep", split_axis=1, concat_axis=0, tiled=True)
     expert_grad = jnp.einsum("es,sfd->efd", old_onehot, arrived, precision=precise)
     new_master, new_moment_one, new_moment_two = adamw(master, moment_one, moment_two, expert_grad)

time: 142 us -> 149 us (1.049)
  the two profiles are of different devices: /device:TPU:8 before, /device:TPU:1 now
where the time goes in v1:
time: 149 us
  blocking collectives  90.2 us (61%)
  matrix products  16.3 us (11%)
  between operations  14.3 us (10%)
  starting transfers between devices  14.1 us (9%)
  local copies, waits for them, and re-layouts  5.36 us (4%)
  waiting for transfers between devices  4.34 us (3%)
  other arithmetic  4.21 us (3%)
    all_to_all x1, blocking collectives, local(): lax.all_to_all(column_grad, 'ep', split_axis=1, concat_axis=0, tiled=True)  53.5 us
    all_to_all x1, blocking collectives, local(): lax.all_to_all(picked, 'ep', split_axis=0, concat_axis=1, tiled=True)  36.8 us
    ppermute x2, starting transfers between devices, local(): from_left = lax.ppermute(from_left, 'dp', ahead)  6.15 us
    all_to_all x1, starting transfers between devices, local(): lax.all_to_all(masked_grads, 'dp', split_axis=2, concat_axis=1, tiled=True)  4.84 us
    dot_general x1, matrix products, local(): jnp.einsum('srf,sfd->srd', masked_acts, whole_weights, precision=precise)  4.76 us
    ppermute x2, waiting for transfers between devices, local(): from_left = lax.ppermute(from_left, 'dp', ahead)  4.32 us
    dot_general x1, matrix products, local(): jnp.einsum('srd,sfd->srf', masked_grads, whole_weights, precision=precise)  3.9 us
    ppermute x1, starting transfers between devices, local(): from_right = lax.ppermute(from_right, 'dp', downward)  3.13 us
  transfers between devices with their start and end apart: 5, of which 2 were waited for; matrix products, arithmetic and copies ran while one was open for 9% of the time, Pallas kernels for 0%

profile of v1, /device:TPU:1, one launch (start us, length us, event | category | flops | bytes accessed | tf_op | source)
XLA Modules:
  0.0 148.9 jit_solution(17490162094817663118)
XLA Ops:
  7.2 0.7 compare_convert_fusion
  7.9 1.0 broadcast_multiply_fusion.1
  9.2 1.3 reshape.38
  10.4 4.8 %all-to-all-start = ((f32[4,1,16384]{2,1,0:T(1,128)}), f32[4,1,16384]{2,1,0:T(1,128)S(1)}, u32[]{:S(2)}, u32[]{:S(2)}) async-start(f32[4,1,16384]{2,1,0:T(1,128)} %reshape.38), calls=%async_computation | async-start | bytes 524288 | tf_op jit(solution)/shard_map/all_to_all | solution.py:46
  15.3 1.1 broadcast_multiply_fusion
  16.4 3.4 %collective-permute-start.1 = (f32[2,64,768]{2,1,0:T(8,128)S(1)}, f32[2,64,768]{2,1,0:T(8,128)S(1)}, u32[]{:S(2)}, u32[]{:S(2)}) collective-permute-start(f32[2,64,768]{2,1,0:T(8,128)S(1)} %broadcast_multiply_fusion), channel_id=1, source_target_pairs={{0,1},{1,2},{2,3},{3,0},{4,5},{5,6},{6,7},{7,4},{8,9},{9,10},{10,1... | collective-permute-start | bytes 1179656 | tf_op jit(solution)/shard_map/ppermute | solution.py:59
  19.8 3.1 %collective-permute-start = (f32[2,64,768]{2,1,0:T(8,128)S(1)}, f32[2,64,768]{2,1,0:T(8,128)S(1)}, u32[]{:S(2)}, u32[]{:S(2)}) collective-permute-start(f32[2,64,768]{2,1,0:T(8,128)S(1)} %broadcast_multiply_fusion), channel_id=1, source_target_pairs={{0,3},{1,0},{2,1},{3,2},{4,7},{5,4},{6,5},{7,6},{8,11},{9,8},{10,9... | collective-permute-start | bytes 1179656 | tf_op jit(solution)/shard_map/ppermute | solution.py:61
  23.0 0.5 broadcast.26
  23.5 1.4 reduce
  25.5 1.4 fusion.11
  27.2 2.8 %collective-permute-start.2 = (f32[2,64,768]{2,1,0:T(8,128)S(1)}, f32[2,64,768]{2,1,0:T(8,128)S(1)}, u32[]{:S(2)}, u32[]{:S(2)}) collective-permute-start(f32[2,64,768]{2,1,0:T(8,128)S(1)} %collective-permute-done.1), channel_id=1, source_target_pairs={{0,1},{1,2},{2,3},{3,0},{4,5},{5,6},{6,7},{7,4},{8,9},{9,10},{10,1... | collective-permute-start | bytes 1179656 | tf_op jit(solution)/shard_map/ppermute | solution.py:59
  30.0 1.4 convolution_add_fusion.2
  31.4 1.4 convolution_add_fusion.1
  32.8 4.0 %collective-permute-done.2 = f32[2,64,768]{2,1,0:T(8,128)S(1)} collective-permute-done((f32[2,64,768]{2,1,0:T(8,128)S(1)}, f32[2,64,768]{2,1,0:T(8,128)S(1)}, u32[]{:S(2)}, u32[]{:S(2)}) %collective-permute-start.2) | collective-permute-done | bytes 393248 | tf_op jit(solution)/shard_map/ppermute | solution.py:59
  36.9 1.4 convolution_add_fusion
  38.3 0.6 copy.33
  38.9 53.5 %all_to_all.54 = f32[2,768,128]{2,0,1:T(2,128)S(1)} all-to-all(f32[2,768,128]{2,0,1:T(2,128)S(1)} %copy.33), channel_id=1, replica_groups=mesh['ep'=128,'dp'=4] {'ep'}, dimensions={1} | all-to-all | bytes 1572864 | tf_op jit(solution)/shard_map/all_to_all | solution.py:79
  92.7 1.5 %multiply_subtract_fusion = (f32[128,6,128]{2,0,1:T(8,128)S(1)}, f32[128,6,128]{2,0,1:T(8,128)}, f32[128,6,128]{2,0,1:T(8,128)}) fusion(f32[128,6,128]{2,0,1:T(8,128)S(1)} %copy-done.2, f32[128,6,128]{2,0,1:T(8,128)S(1)} %copy-done.3, f32[128,6,128]{2,0,1:T(8,128)S(1)} %copy-done.4, f32[256,6,128]{2,0,1:T(8,128)S(1)} %bitcast.38, s32[256]{0:T(256)S(1)} %bitcast.45), kind=kOutput, calls=%fused_computation.5 | convolution fusion | flops 303497216 | bytes 3146752 | tf_op jit(solution)/shard_map/es,sfd->efd/dot_general | solution.py:80
  94.3 0.5 fusion.5
  94.8 0.5 copy.35
  95.3 36.8 %all_to_all.55 = f32[256,6,128]{2,1,0:T(8,128)S(1)} all-to-all(f32[256,6,128]{2,1,0:T(8,128)S(1)} %copy.35), channel_id=1, replica_groups=mesh['ep'=128,'dp'=4] {'ep'}, dimensions={0} | all-to-all | bytes 1572864 | tf_op jit(solution)/shard_map/all_to_all | solution.py:84
  132.5 0.9 copy.37
  133.4 4.8 %fusion.19 = f32[2,64,512]{2,1,0:T(8,128)} fusion(f32[2,64,768]{2,1,0:T(8,128)S(1)} %broadcast_multiply_fusion, f32[2,768,512]{2,1,0:T(8,128)} %all-gather.2.cloned.1.call-done), kind=kOutput, calls=%fused_computation.27 | convolution fusion | flops 603979776 | bytes 3801088 | tf_op jit(solution)/shard_map/srf,sfd->srd/dot_general | solution.py:44
  138.2 3.9 %fusion.20 = f32[2,64,768]{2,1,0:T(8,128)} fusion(f32[2,64,512]{2,1,0:T(8,128)S(1)} %broadcast_multiply_fusion.1, f32[2,768,512]{2,1,0:T(8,128)S(1)} %copy-done), kind=kOutput, calls=%fused_computation.28 | convolution fusion | flops 603979776 | bytes 3801088 | tf_op jit(solution)/shard_map/srd,sfd->srf/dot_general | solution.py:45
  (25 shorter events, 1.9 us)
Async XLA Ops:
  10.4 12.5 %all-to-all-start = ((f32[4,1,16384]{2,1,0:T(1,128)}), f32[4,1,16384]{2,1,0:T(1,128)S(1)}, u32[]{:S(2)}, u32[]{:S(2)}) async-start(f32[4,1,16384]{2,1,0:T(1,128)} %reshape.38), calls=%async_computation | async-start | bytes 524288 | tf_op jit(solution)/shard_map/all_to_all | solution.py:46
  15.3 118.1 %all-gather.2.cloned.1.call-start = ((), (), s32[]{:S(2)}) async-start(), calls=%async_computation.3 | async-start | bytes 3932160 | tf_op jit(solution)/shard_map/all_gather | solution.py:43
  16.4 10.8 %collective-permute-start.1 = (f32[2,64,768]{2,1,0:T(8,128)S(1)}, f32[2,64,768]{2,1,0:T(8,128)S(1)}, u32[]{:S(2)}, u32[]{:S(2)}) collective-permute-start(f32[2,64,768]{2,1,0:T(8,128)S(1)} %broadcast_multiply_fusion), channel_id=1, source_target_pairs={{0,1},{1,2},{2,3},{3,0},{4,5},{5,6},{6,7},{7,4},{8,9},{9,10},{10,1... | collective-permute-start | bytes 1179656 | tf_op jit(solution)/shard_map/ppermute | solution.py:59
  19.8 10.2 %collective-permute-start = (f32[2,64,768]{2,1,0:T(8,128)S(1)}, f32[2,64,768]{2,1,0:T(8,128)S(1)}, u32[]{:S(2)}, u32[]{:S(2)}) collective-permute-start(f32[2,64,768]{2,1,0:T(8,128)S(1)} %broadcast_multiply_fusion), channel_id=1, source_target_pairs={{0,3},{1,0},{2,1},{3,2},{4,7},{5,4},{6,5},{7,6},{8,11},{9,8},{10,9... | collective-permute-start | bytes 1179656 | tf_op jit(solution)/shard_map/ppermute | solution.py:61
  27.2 9.7 %collective-permute-start.2 = (f32[2,64,768]{2,1,0:T(8,128)S(1)}, f32[2,64,768]{2,1,0:T(8,128)S(1)}, u32[]{:S(2)}, u32[]{:S(2)}) collective-permute-start(f32[2,64,768]{2,1,0:T(8,128)S(1)} %collective-permute-done.1), channel_id=1, source_target_pairs={{0,1},{1,2},{2,3},{3,0},{4,5},{5,6},{6,7},{7,4},{8,9},{9,10},{10,1... | collective-permute-start | bytes 1179656 | tf_op jit(solution)/shard_map/ppermute | solution.py:59
  32.8 59.9 %copy-start.2 = (f32[128,6,128]{2,0,1:T(8,128)S(1)}, f32[128,6,128]{2,0,1:T(8,128)}, u32[]{:S(2)}) copy-start(f32[128,6,128]{2,0,1:T(8,128)} %param.13) | copy-start | bytes 1179652
  32.8 59.9 %copy-start.3 = (f32[128,6,128]{2,0,1:T(8,128)S(1)}, f32[128,6,128]{2,0,1:T(8,128)}, u32[]{:S(2)}) copy-start(f32[128,6,128]{2,0,1:T(8,128)} %param.14) | copy-start | bytes 1179652
  32.8 59.9 %copy-start.4 = (f32[128,6,128]{2,0,1:T(8,128)S(1)}, f32[128,6,128]{2,0,1:T(8,128)}, u32[]{:S(2)}) copy-start(f32[128,6,128]{2,0,1:T(8,128)} %param.15) | copy-start | bytes 1179652
  32.8 59.9 %copy-start.5 = (s32[256,1]{0,1:T(1,128)S(1)}, s32[256,1]{0,1:T(1,128)}, u32[]{:S(2)}) copy-start(s32[256,1]{0,1:T(1,128)} %param.16) | copy-start | bytes 3076
  38.9 55.3 %copy-start.6 = (s32[256,1]{0,1:T(1,128)S(1)}, s32[256,1]{0,1:T(1,128)}, u32[]{:S(2)}) copy-start(s32[256,1]{0,1:T(1,128)} %param.17) | copy-start | bytes 3076
  94.3 38.2 %copy-start.1 = (f32[128,6,128]{2,0,1:T(8,128)}, f32[128,6,128]{2,0,1:T(8,128)S(1)}, u32[]{:S(2)}) copy-start(f32[128,6,128]{2,0,1:T(8,128)S(1)} %get-tuple-element.24) | copy-start | bytes 1179652
  133.4 4.8 %copy-start = (f32[2,768,512]{2,1,0:T(8,128)S(1)}, f32[2,768,512]{2,1,0:T(8,128)}, u32[]{:S(2)}) copy-start(f32[2,768,512]{2,1,0:T(8,128)} %all-gather.2.cloned.1.call-done) | copy-start | bytes 9437188
Sparse Core Ops, SparseCore 0:
  23.0 52.4 all-gather.1
